TPU v7x, 32 devices: a whole 2x2x4 slice. The times are simulated.
32 devices in a mesh: blk: 4 (over y, core), group: 8 (over z, x).
Axes of the slice: x: 2, y: 2, z: 4, core: 2. Of those that a mesh axis runs over, the one named last changes fastest.
Arguments:
- queries: bfloat16 [32, 16, 128], P(('blk', 'group')), may hold values from -2.5 to 2.5
- query_mask: int32 [32, 16], P(('blk', 'group')), may hold values from 0 to 1, as said below
- positive: int32 [32], P(('blk', 'group')), may hold values from 0 to 63
- page_vectors: bfloat16 [64, 128, 128], P(('blk', 'group')), may hold values from -2 to 2
- page_mask: int32 [64, 128], P(('blk', 'group')), may hold values from 0 to 1, as said below
Outputs:
- grad_queries: float32 [32, 16, 128], P(('blk', 'group'))
- grad_pages: float32 [64, 128, 128], P(('blk', 'group'))
- mean_loss: float32 [], replicated
Inputs may be any that keep to these rules, and one draw needn't show every extreme that they name: `query_mask`: each row holds ones on its first 8 to 16 token slots and zeros after them. `page_mask`: each row holds ones on its first 32 to 128 patch slots and zeros after them.
All inputs are finite; a program needn't handle non-finite values.
Results may differ from a plain program's by a relative error of at most 0.0028.
Values may be sent and summed in bfloat16 or wider, within the bound.
No kernel may reach another device: no remote copies, remote signals or barrier semaphores. Data moves between devices by JAX's collectives and lax.ppermute only.
A program may use at most 64 MiB of HBM per device.

v0:
```python
import math
import jax
import jax.numpy as jnp
from jax import lax
from jax.sharding import PartitionSpec as P

relaxation_scale_factor = 0.5
guarded_floor_entry = -1e30


def combined_all(part, axis, combine):
    gathered = jax.tree.map(lambda a: lax.all_gather(a, axis), part)

    def take(source):
        return jax.tree.map(lambda a: lax.dynamic_index_in_dim(a, source, 0, False), gathered)

    return lax.fori_loop(
        1, lax.axis_size(axis), lambda source, state: combine(state, take(source)), take(0)
    )


def from_behind(value, axis, steps):
    count = lax.axis_size(axis)
    pairs = [(source, (source + steps) % count) for source in range(count)]
    return lax.ppermute(value, axis, pairs)


def masked_logits(row_block, lone_document, live_image_embeddings):
    similarity_matrix = lax.dot_general(
        row_block, lone_document, (((1,), (1,)), ((), ())), preferred_element_type=jnp.float32
    )
    return jnp.where(
        live_image_embeddings[None, :] > 0,
        similarity_matrix / relaxation_scale_factor,
        guarded_floor_entry,
    )


def combine_parts(earlier, later):
    highest = jnp.maximum(earlier[0], later[0])
    totals = earlier[1] * jnp.exp(earlier[0] - highest) + later[1] * jnp.exp(later[0] - highest)
    return (highest, totals, earlier[2] + later[2])


def on_device(queries, query_mask, positive, page_vectors, page_mask):
    tokens = queries.shape[1]
    features = queries.shape[2]
    local_pages = page_vectors.shape[0]
    blocks = lax.axis_size("blk")
    members = lax.axis_size("group")
    bundle_size = queries.shape[0] * members
    total_queries = bundle_size * blocks
    natural_logarithm_lengths = jnp.log(jnp.sum(page_mask.astype(jnp.float32), axis=1))
    bundle_vectors, bundle_masks, bundle_targets = (
        lax.all_gather(queries, "group", axis=0, tiled=True),
        lax.all_gather(query_mask, "group", axis=0, tiled=True),
        lax.all_gather(positive, "group", axis=0, tiled=True),
    )

    def forward_piece(folded, shard_in, root_row):
        scores, lse_rows, live_all, owners, kept = folded
        vectors, token_masks, targets = shard_in
        amount = vectors.shape[0]
        stride = math.gcd(amount, max(1, 512 // tokens))

        def run_block(number, current):
            scores, lse_rows = current
            offset = number * stride
            slab_rows = lax.dynamic_slice_in_dim(vectors, offset, stride, 0).reshape(
                stride * tokens, features
            )
            alive = lax.dynamic_slice_in_dim(token_masks, offset, stride, 0).astype(jnp.float32)
            found_sums = []
            for index_page in range(local_pages):
                masked = masked_logits(slab_rows, page_vectors[index_page], page_mask[index_page])
                highest = jnp.max(masked, axis=1, keepdims=True)
                found_sums.append(
                    highest[:, 0] + jnp.log(jnp.sum(jnp.exp(masked - highest), axis=1))
                )
            logsumexp_results = jnp.stack(found_sums, axis=1).reshape(stride, tokens, local_pages)
            softened_supremum = relaxation_scale_factor * (
                logsumexp_results - natural_logarithm_lengths
            )
            page_score = jnp.sum(alive[:, :, None] * softened_supremum, axis=1)
            scores = lax.dynamic_update_slice_in_dim(scores, page_score, offset, 0)
            lse_rows = lax.dynamic_update_slice_in_dim(lse_rows, logsumexp_results, offset, 0)
            return (scores, lse_rows)

        scores, lse_rows = lax.fori_loop(0, amount // stride, run_block, (scores, lse_rows))
        live_all = lax.dynamic_update_slice_in_dim(live_all, token_masks, root_row, 0)
        owners = lax.dynamic_update_slice_in_dim(owners, targets, root_row, 0)
        kept = vectors
        return (scores, lse_rows, live_all, owners, kept)

    starting = (
        jnp.zeros((total_queries, local_pages), jnp.float32),
        jnp.zeros((total_queries, tokens, local_pages), jnp.float32),
        jnp.zeros((total_queries, tokens), jnp.int32),
        jnp.zeros((total_queries,), jnp.int32),
        jnp.zeros((total_queries, tokens, features), jnp.bfloat16),
    )
    scores, lse_rows, live_all, owners, kept = forward_piece(
        starting,
        (
            lax.all_gather(bundle_vectors, "blk", axis=0, tiled=True),
            lax.all_gather(bundle_masks, "blk", axis=0, tiled=True),
            lax.all_gather(bundle_targets, "blk", axis=0, tiled=True),
        ),
        jnp.int32(0),
    )
    position = lax.axis_index(("blk", "group"))
    page_ids = position * local_pages + jnp.arange(local_pages, dtype=jnp.int32)
    chosen = owners[:, None] == page_ids[None, :]
    picked_local = jnp.sum(jnp.where(chosen, scores, 0.0))
    local_top = jnp.max(scores, axis=1)
    local_total = jnp.sum(jnp.exp(scores - local_top[:, None]), axis=1)
    highest, totals, picked = combined_all(
        (local_top, local_total, picked_local), ("blk", "group"), combine_parts
    )
    page_lse = highest + jnp.log(totals)
    mean_loss = (jnp.sum(page_lse) - picked) / total_queries
    coefficient = jnp.exp(scores - page_lse[:, None]) - chosen.astype(jnp.float32)
    factor_scale = coefficient[:, None, :] * live_all.astype(jnp.float32)[:, :, None]

    def slice_rows(root_row, amount):
        sums = lax.dynamic_slice_in_dim(lse_rows, root_row, amount, 0).reshape(
            amount * tokens, local_pages
        )
        scales = lax.dynamic_slice_in_dim(factor_scale, root_row, amount, 0).reshape(
            amount * tokens, local_pages
        )
        return (sums, scales)

    def gradient_terms(row_block, logsumexp_results, scales, page_grads):
        partial_value = jnp.zeros(row_block.shape, jnp.float32)
        for number in range(local_pages):
            masked = masked_logits(row_block, page_vectors[number], page_mask[number])
            weights = jnp.exp(masked - logsumexp_results[:, number : number + 1])
            factor = (scales[:, number : number + 1] * weights).astype(jnp.bfloat16)
            partial_value = partial_value + jnp.dot(
                factor, page_vectors[number], preferred_element_type=jnp.float32
            )
            update = lax.dot_general(
                factor, row_block, (((0,), (0,)), ((), ())), preferred_element_type=jnp.float32
            )
            page_grads = page_grads.at[number].add(update)
        return (partial_value, page_grads)

    home = lax.axis_index("blk")
    page_grads = jnp.zeros(page_vectors.shape, jnp.float32)

    def visit_one(moving, collected, page_grads, lap_index):
        root_row = (home - lap_index) % blocks * bundle_size
        sums, scales = slice_rows(root_row, bundle_size)
        partial_value, page_grads = gradient_terms(
            moving.reshape(bundle_size * tokens, features), sums, scales, page_grads
        )
        return (collected + partial_value.reshape(bundle_size, tokens, features), page_grads)

    def pass_one(collected):
        return from_behind(collected, "blk", 1)

    def turn_one(lap_index, current):
        moving, collected, page_grads = current
        collected, page_grads = visit_one(moving, collected, page_grads, lap_index)
        moving = from_behind(moving, "blk", 1)
        return (moving, pass_one(collected), page_grads)

    empty_whole = jnp.zeros((bundle_size, tokens, features), jnp.float32)
    moving, collected, page_grads = lax.fori_loop(
        0, blocks - 1, turn_one, (bundle_vectors, empty_whole, page_grads)
    )
    collected, page_grads = visit_one(moving, collected, page_grads, blocks - 1)
    collected = pass_one(collected)
    grad_queries = lax.psum_scatter(collected, "group", scatter_dimension=0, tiled=True)
    return (grad_queries, page_grads, mean_loss)


def solution(mesh):
    in_specs = (
        P(("blk", "group"), None, None),
        P(("blk", "group"), None),
        P(("blk", "group")),
        P(("blk", "group"), None, None),
        P(("blk", "group"), None),
    )
    out_specs = (P(("blk", "group"), None, None), P(("blk", "group"), None, None), P())
    return jax.shard_map(
        on_device, mesh=mesh, in_specs=in_specs, out_specs=out_specs, check_vma=False
    )
```

profile of v0, /device:TPU:0, one launch (start us, length us, event | category | flops | bytes accessed | tf_op | source)
XLA Modules:
  0.0 262.9 jit_solution(15310981650806206361)
XLA Ops:
  7.2 0.8 compare_bitcast_fusion.2
  8.1 32.4 %all_gather.36 = bf16[8,16,128]{2,1,0:T(8,128)(2,1)S(1)} all-gather(bf16[1,16,128]{2,1,0:T(8,128)(2,1)S(1)} %copy-done.4), channel_id=1, replica_groups=mesh['blk'=4,'group'=8] {'group'}, dimensions={0}, use_global_device_ids=true | all-gather | bytes 36864 | tf_op jit(solution)/shard_map/all_gather | solution.py:55
  40.6 5.5 %all_gather.37 = bf16[32,16,128]{2,1,0:T(8,128)(2,1)S(1)} all-gather(bf16[8,16,128]{2,1,0:T(8,128)(2,1)S(1)} %all_gather.36), channel_id=1, replica_groups=mesh['blk'=4,'group'=8] {'blk'}, dimensions={0}, use_global_device_ids=true | all-gather | bytes 163840 | tf_op jit(solution)/shard_map/all_gather | solution.py:105
  46.8 0.7 copy-done.5
  47.5 20.4 %all-gather.2 = s32[8,1,16]{2,1,0:T(1,128)S(1)} all-gather(s32[1,1,16]{2,1,0:T(1,128)S(1)} %bitcast.182), channel_id=1, replica_groups=mesh['blk'=4,'group'=8] {'group'}, dimensions={0}, use_global_device_ids=true | all-gather | bytes 576 | tf_op jit(solution)/shard_map/all_gather | solution.py:56
  67.9 5.2 %all_gather.39 = s32[32,16]{1,0:T(8,128)S(1)} all-gather(s32[8,16]{1,0:T(8,128)S(1)} %bitcast.181), channel_id=1, replica_groups=mesh['blk'=4,'group'=8] {'blk'}, dimensions={0}, use_global_device_ids=true | all-gather | bytes 2560 | tf_op jit(solution)/shard_map/all_gather | solution.py:106
  73.1 0.7 copy-done.7
  75.0 0.8 dynamic-update-slice.28
  75.8 6.8 %all-reduce.2 = s32[8]{0:T(128)S(1)} all-reduce(s32[8]{0:T(128)S(1)} %dynamic-update-slice.28), channel_id=1, replica_groups=mesh['blk'=4,'group'=8] {'group'}, use_global_device_ids=true, to_apply=%add.2 | all-reduce | flops 8 | bytes 64
  84.1 4.9 %all-reduce.3 = s32[32]{0:T(128)S(1)} all-reduce(s32[32]{0:T(128)S(1)} %dynamic-update-slice.29), channel_id=1, replica_groups=mesh['blk'=4,'group'=8] {'blk'}, use_global_device_ids=true, to_apply=%add.3 | all-reduce | flops 32 | bytes 256
  89.2 0.7 fusion.54
  90.3 0.8 dynamic-update-slice.30
  91.0 40.5 %all-reduce.5 = (f32[1024]{0:T(1024)S(1)}, f32[1024]{0:T(1024)S(1)}, f32[32]{0:T(128)S(1)}) all-reduce(f32[1024]{0:T(1024)S(1)} %dynamic-update-slice.26, f32[1024]{0:T(1024)S(1)} %dynamic-update-slice.27, f32[32]{0:T(128)S(1)} %dynamic-update-slice.30), channel_id=2, replica_groups=mesh['blk'=4,'group'=8] {'blk','group'}, use_global_device_ids=true, to_apply=%add | all-reduce | flops 2080 | bytes 16640
  131.7 39.9 %while.48 = (s32[]{:T(128)}, f32[32]{0:T(128)S(1)}, f32[32]{0:T(128)S(1)}, f32[]{:T(128)}, f32[32,32]{1,0:T(8,128)S(1)}, /*index=5*/f32[32,32]{1,0:T(8,128)S(1)}, f32[32]{0:T(128)S(1)}, s32[]{:T(128)}, s32[]{:T(128)}, s32[]{:T(128)}) while((s32[]{:T(128)}, f32[32]{0:T(128)S(1)}, f32[32]{0:T(128)S(1)}, f32[]{:T(128)}, ...), condition=%wide.region_10.11_spmd, body=%wide.region_9.10_spmd.sunk | while | flops 198 | bytes 939 | solution.py:17
  131.7 0.6 dynamic_slice.91
  133.0 0.6 dynamic_slice.91
  134.3 0.6 dynamic_slice.91
  135.6 0.6 dynamic_slice.91
  136.9 0.6 dynamic_slice.91
  138.2 0.6 dynamic_slice.91
  139.5 0.6 dynamic_slice.91
  140.8 0.6 dynamic_slice.91
  142.0 0.6 dynamic_slice.91
  143.3 0.6 dynamic_slice.91
  144.6 0.6 dynamic_slice.91
  145.9 0.6 dynamic_slice.91
  147.2 0.6 dynamic_slice.91
  148.5 0.6 dynamic_slice.91
  149.8 0.6 dynamic_slice.91
  151.1 0.6 dynamic_slice.91
  152.4 0.6 dynamic_slice.91
  153.6 0.6 dynamic_slice.91
  154.9 0.6 dynamic_slice.91
  156.2 0.6 dynamic_slice.91
  157.5 0.6 dynamic_slice.91
  158.8 0.6 dynamic_slice.91
  170.4 0.6 dynamic_slice.91
  171.6 0.6 fusion.56
  172.6 13.9 %while.49 = (s32[]{:T(128)}, bf16[8,16,128]{2,1,0:T(8,128)(2,1)S(1)}, f32[8,16,128]{2,1,0:T(8,128)S(1)}, f32[2,128,128]{2,1,0:T(8,128)S(1)}, s32[]{:T(128)}, /*i...) while((s32[]{:T(128)}, ...), condition=%wide.region_12.13_spmd, body=%wide.region_11.12_spmd.sunk | while | flops 25395472 | bytes 1589896 | solution.py:170
  173.6 2.4 collective-permute-start.1
  176.4 0.9 collective-permute-done.1
  178.2 2.4 collective-permute-start.1
  181.0 0.9 collective-permute-done.1
  182.8 2.4 collective-permute-start.1
  185.6 0.9 collective-permute-done.1
  188.1 2.8 %collective-permute-done.2 = f32[8,16,128]{2,1,0:T(8,128)S(1)} collective-permute-done((f32[8,16,128]{2,1,0:T(8,128)S(1)}, f32[8,16,128]{2,1,0:T(8,128)S(1)}, u32[]{:S(2)}, u32[]{:S(2)}) %collective-permute-start.2) | collective-permute-done | bytes 65568 | tf_op jit(solution)/shard_map/ppermute | solution.py:25
  190.9 0.6 copy-done.2
  191.8 63.1 %reduce-scatter.2.cloned.1.call-done = f32[1,16,128]{2,1,0:T(8,128)} async-done(((f32[8,16,128]{2,1,0:T(8,128)}), f32[1,16,128]{2,1,0:T(8,128)}) %reduce-scatter.2.cloned.1.call-update) | async-done | bytes 8208 | tf_op jit(solution)/shard_map/reduce_scatter | solution.py:175
  (150 shorter events, 13.6 us)
Async XLA Ops:
  7.2 0.8 copy-start.3
  7.2 0.9 copy-start.4
  7.2 247.7 %reduce-scatter.2.cloned.1.call-start = ((), (), s32[]{:S(2)}) async-start(), calls=%async_computation.1 | async-start | bytes 73728 | tf_op jit(solution)/shard_map/reduce_scatter | solution.py:175
  40.5 5.5 %copy-start.1 = (bf16[2,128,128]{2,1,0:T(8,128)(2,1)S(1)}, bf16[2,128,128]{2,1,0:T(8,128)(2,1)}, u32[]{:S(2)}) copy-start(bf16[2,128,128]{2,1,0:T(8,128)(2,1)} %param.20) | copy-start | bytes 196612
  46.8 0.7 copy-start.5
  73.1 0.7 copy-start.7
  75.8 6.8 %copy-start.6 = (u32[32]{0:T(128)S(1)}, u32[32]{0:T(128)}, u32[]{:S(2)}) copy-start(u32[32]{0:T(128)} %constant.385) | copy-start | bytes 388
  172.6 3.7 %collective-permute-start = (bf16[8,16,128]{2,1,0:T(8,128)(2,1)S(1)}, bf16[8,16,128]{2,1,0:T(8,128)(2,1)S(1)}, u32[]{:S(2)}, u32[]{:S(2)}) collective-permute-start(bf16[8,16,128]{2,1,0:T(8,128)(2,1)S(1)} %copy.33), channel_id=1, source_target_pairs={{0,8},{8,16},{16,24},{24,0},{1,9},{9,17},{17,25},{25,1},{2,10},{10... | collective-permute-start | bytes 98312 | tf_op jit(solution)/shard_map/while/body/eval_jaxpr/ppermute | solution.py:25
  173.6 3.7 %collective-permute-start.1 = (f32[8,16,128]{2,1,0:T(8,128)S(1)}, f32[8,16,128]{2,1,0:T(8,128)S(1)}, u32[]{:S(2)}, u32[]{:S(2)}) collective-permute-start(f32[8,16,128]{2,1,0:T(8,128)S(1)} %add.305), channel_id=1, source_target_pairs={{0,8},{8,16},{16,24},{24,0},{1,9},{9,17},{17,25},{25,1},{2,10},{10... | collective-permute-start | bytes 196616 | tf_op jit(solution)/shard_map/while/body/eval_jaxpr/ppermute | solution.py:25
  177.3 3.7 %collective-permute-start = (bf16[8,16,128]{2,1,0:T(8,128)(2,1)S(1)}, bf16[8,16,128]{2,1,0:T(8,128)(2,1)S(1)}, u32[]{:S(2)}, u32[]{:S(2)}) collective-permute-start(bf16[8,16,128]{2,1,0:T(8,128)(2,1)S(1)} %copy.33), channel_id=1, source_target_pairs={{0,8},{8,16},{16,24},{24,0},{1,9},{9,17},{17,25},{25,1},{2,10},{10... | collective-permute-start | bytes 98312 | tf_op jit(solution)/shard_map/while/body/eval_jaxpr/ppermute | solution.py:25
  178.2 3.7 %collective-permute-start.1 = (f32[8,16,128]{2,1,0:T(8,128)S(1)}, f32[8,16,128]{2,1,0:T(8,128)S(1)}, u32[]{:S(2)}, u32[]{:S(2)}) collective-permute-start(f32[8,16,128]{2,1,0:T(8,128)S(1)} %add.305), channel_id=1, source_target_pairs={{0,8},{8,16},{16,24},{24,0},{1,9},{9,17},{17,25},{25,1},{2,10},{10... | collective-permute-start | bytes 196616 | tf_op jit(solution)/shard_map/while/body/eval_jaxpr/ppermute | solution.py:25
  182.0 3.6 %collective-permute-start = (bf16[8,16,128]{2,1,0:T(8,128)(2,1)S(1)}, bf16[8,16,128]{2,1,0:T(8,128)(2,1)S(1)}, u32[]{:S(2)}, u32[]{:S(2)}) collective-permute-start(bf16[8,16,128]{2,1,0:T(8,128)(2,1)S(1)} %copy.33), channel_id=1, source_target_pairs={{0,8},{8,16},{16,24},{24,0},{1,9},{9,17},{17,25},{25,1},{2,10},{10... | collective-permute-start | bytes 98312 | tf_op jit(solution)/shard_map/while/body/eval_jaxpr/ppermute | solution.py:25
  182.8 3.7 %collective-permute-start.1 = (f32[8,16,128]{2,1,0:T(8,128)S(1)}, f32[8,16,128]{2,1,0:T(8,128)S(1)}, u32[]{:S(2)}, u32[]{:S(2)}) collective-permute-start(f32[8,16,128]{2,1,0:T(8,128)S(1)} %add.305), channel_id=1, source_target_pairs={{0,8},{8,16},{16,24},{24,0},{1,9},{9,17},{17,25},{25,1},{2,10},{10... | collective-permute-start | bytes 196616 | tf_op jit(solution)/shard_map/while/body/eval_jaxpr/ppermute | solution.py:25
  187.2 3.7 %collective-permute-start.2 = (f32[8,16,128]{2,1,0:T(8,128)S(1)}, f32[8,16,128]{2,1,0:T(8,128)S(1)}, u32[]{:S(2)}, u32[]{:S(2)}) collective-permute-start(f32[8,16,128]{2,1,0:T(8,128)S(1)} %add.250), channel_id=1, source_target_pairs={{0,8},{8,16},{16,24},{24,0},{1,9},{9,17},{17,25},{25,1},{2,10},{10... | collective-permute-start | bytes 196616 | tf_op jit(solution)/shard_map/ppermute | solution.py:25
  190.9 0.6 copy-start.2
  191.8 63.1 %copy-start = (f32[2,128,128]{2,1,0:T(8,128)}, f32[2,128,128]{2,1,0:T(8,128)S(1)}, u32[]{:S(2)}) copy-start(f32[2,128,128]{2,1,0:T(8,128)S(1)} %fusion.38) | copy-start | bytes 393220
Sparse Core Ops, SparseCore 0:
  191.7 63.1 reduce-scatter.1
where the time goes:
time: 264 us; the launch traced here: 263 us
  blocking collectives  116 us (44%)
  waiting for transfers between devices  68.8 us (26%)
  local copies, waits for them, and re-layouts  24.5 us (9%)
  loops' own time  21.1 us (8%)
  between operations  17.3 us (7%)
  starting transfers between devices  7.44 us (3%)
  matrix products  4.3 us (2%)
  other arithmetic  3.58 us (1%)
    reduce_scatter x1, waiting for transfers between devices, on_device(): lax.psum_scatter(collected, 'group', scatter_dimension=0, tiled=True)  63.1 us
    unnamed x3, blocking collectives  52.2 us
    all_gather x1, blocking collectives, on_device(): lax.all_gather(queries, 'group', axis=0, tiled=True)  32.4 us
    another operation x1, loops' own time, combined_all(): lax.fori_loop(1, lax.axis_size(axis), lambda source, state: combine(state...  20.9 us
    all_gather x1, blocking collectives, on_device(): lax.all_gather(query_mask, 'group', axis=0, tiled=True)  20.4 us
    dynamic_slice x33, local copies, waits for them, and re-layouts, take(): lax.dynamic_index_in_dim(a, source, 0, False)  18.2 us
    ppermute x7, starting transfers between devices, from_behind(): return lax.ppermute(value, axis, pairs)  7.4 us
    ppermute x7, waiting for transfers between devices, from_behind(): return lax.ppermute(value, axis, pairs)  5.66 us
  transfers between devices with their start and end apart: 8, of which 5 were waited for; matrix products, arithmetic and copies ran while one was open for 1% of the time, Pallas kernels for 0%

commit v1 on v0

--- a/solution.py
+++ b/solution.py
@@ -6,6 +6,28 @@
 
 relaxation_scale_factor = 0.5
 guarded_floor_entry = -1e30
+
+
+def laid_out(pieces, dim):
+    pieces = jnp.moveaxis(pieces, 0, dim)
+    shape = pieces.shape
+    return pieces.reshape(*shape[:dim], shape[dim] * shape[dim + 1], *shape[dim + 2 :])
+
+
+def collected_by_bits(x, axis):
+    size = lax.axis_size(axis)
+    pieces = x[None]
+    for level in range(size.bit_length() - 1):
+        bit = 1 << level
+        partner_block = lax.ppermute(pieces, axis, [(i, i ^ bit) for i in range(size)])
+        both = jnp.stack([pieces, partner_block])
+        upper = lax.axis_index(axis) >> level & 1
+        pieces = jnp.where(upper == 0, both, both[::-1]).reshape(-1, *x.shape)
+    return pieces
+
+
+def doubled_up(x, axis, dim):
+    return laid_out(collected_by_bits(x, axis), dim)
 
 
 def combined_all(part, axis, combine):
@@ -53,7 +75,7 @@
     natural_logarithm_lengths = jnp.log(jnp.sum(page_mask.astype(jnp.float32), axis=1))
     bundle_vectors, bundle_masks, bundle_targets = (
         lax.all_gather(queries, "group", axis=0, tiled=True),
-        lax.all_gather(query_mask, "group", axis=0, tiled=True),
+        doubled_up(query_mask, "group", 0),
         lax.all_gather(positive, "group", axis=0, tiled=True),
     )
 

time: 264 us -> 249 us (0.943)
  blocking collectives: 116 us -> 94.8 us
  starting transfers between devices: 7.44 us -> 13 us
    all_gather x1 -> x0, blocking collectives: 20.4 us -> none  [on_device(): lax.all_gather(query_mask, 'group', axis=0, tiled=True)]
    ppermute x0 -> x3, starting transfers between devices: none -> 5.58 us  [collected_by_bits(): lax.ppermute(pieces, axis, [(i, i ^ bit) for i in range(size)])]
  transfers between devices with their start and end apart: 8 -> 11, of which waited for: 5 -> 5; matrix products, arithmetic and copies ran while one was open for 1% -> 3% of each run, Pallas kernels for 0% -> 0%
where the time goes in v1:
time: 249 us; the launch traced here: 248 us
  blocking collectives  94.8 us (38%)
  waiting for transfers between devices  69 us (28%)
  local copies, waits for them, and re-layouts  25.2 us (10%)
  loops' own time  21.1 us (8%)
  between operations  17.3 us (7%)
  starting transfers between devices  13 us (5%)
  matrix products  4.3 us (2%)
  other arithmetic  3 us (1%)
    reduce_scatter x1, waiting for transfers between devices, on_device(): lax.psum_scatter(collected, 'group', scatter_dimension=0, tiled=True)  63.4 us
    unnamed x3, blocking collectives  53.2 us
    all_gather x1, blocking collectives, on_device(): lax.all_gather(queries, 'group', axis=0, tiled=True)  30.9 us
    another operation x1, loops' own time, combined_all(): lax.fori_loop(1, lax.axis_size(axis), lambda source, state: combine(state...  20.9 us
    dynamic_slice x33, local copies, waits for them, and re-layouts, take(): lax.dynamic_index_in_dim(a, source, 0, False)  18.2 us
    ppermute x7, starting transfers between devices, from_behind(): return lax.ppermute(value, axis, pairs)  7.4 us
    unnamed x29, local copies, waits for them, and re-layouts  5.99 us
    ppermute x7, waiting for transfers between devices, from_behind(): return lax.ppermute(value, axis, pairs)  5.66 us
  transfers between devices with their start and end apart: 11, of which 5 were waited for; matrix products, arithmetic and copies ran while one was open for 3% of the time, Pallas kernels for 0%

profile of v1, /device:TPU:0, one launch (start us, length us, event | category | flops | bytes accessed | tf_op | source)
XLA Modules:
  0.0 247.9 jit_solution(8727537257648169158)
XLA Ops:
  7.2 0.6 copy-done.5
  7.8 3.0 %collective-permute-start.2 = (s32[1,1,16]{2,1,0:T(1,128)S(1)}, s32[1,1,16]{2,1,0:T(1,128)S(1)}, u32[]{:S(2)}, u32[]{:S(2)}) collective-permute-start(s32[1,1,16]{2,1,0:T(1,128)S(1)} %bitcast.196), channel_id=1, source_target_pairs={{0,1},{1,0},{2,3},{3,2},{4,5},{5,4},{6,7},{7,6},{8,9},{9,8},{10,11... | collective-permute-start | bytes 200 | tf_op jit(solution)/shard_map/ppermute | solution.py:22
  11.0 0.7 copy-done.4
  11.6 30.9 %all_gather.33 = bf16[8,16,128]{2,1,0:T(8,128)(2,1)S(1)} all-gather(bf16[1,16,128]{2,1,0:T(8,128)(2,1)S(1)} %copy-done.4), channel_id=1, replica_groups=mesh['blk'=4,'group'=8] {'group'}, dimensions={0}, use_global_device_ids=true | all-gather | bytes 36864 | tf_op jit(solution)/shard_map/all_gather | solution.py:77
  42.6 5.5 %all_gather.34 = bf16[32,16,128]{2,1,0:T(8,128)(2,1)S(1)} all-gather(bf16[8,16,128]{2,1,0:T(8,128)(2,1)S(1)} %all_gather.33), channel_id=1, replica_groups=mesh['blk'=4,'group'=8] {'blk'}, dimensions={0}, use_global_device_ids=true | all-gather | bytes 163840 | tf_op jit(solution)/shard_map/all_gather | solution.py:127
  48.9 0.6 copy-done.7
  49.5 0.7 dynamic-slice.50
  51.5 0.8 dynamic-update-slice.28
  52.9 10.0 %all-reduce.2 = s32[8]{0:T(128)S(1)} all-reduce(s32[8]{0:T(128)S(1)} %dynamic-update-slice.28), channel_id=1, replica_groups=mesh['blk'=4,'group'=8] {'group'}, use_global_device_ids=true, to_apply=%add.2 | all-reduce | flops 8 | bytes 64
  62.9 2.5 %collective-permute-start.4 = (s32[4,1,16]{2,0,1:T(4,128)S(1)}, s32[4,1,16]{2,0,1:T(4,128)S(1)}, u32[]{:S(2)}, u32[]{:S(2)}) collective-permute-start(s32[4,1,16]{2,0,1:T(4,128)S(1)} %bitcast.190), channel_id=1, source_target_pairs={{0,4},{1,5},{2,6},{3,7},{4,0},{5,1},{6,2},{7,3},{8,12},{9,13},{10,... | collective-permute-start | bytes 776 | tf_op jit(solution)/shard_map/ppermute | solution.py:22
  65.6 4.9 %all-reduce.3 = s32[32]{0:T(128)S(1)} all-reduce(s32[32]{0:T(128)S(1)} %dynamic-update-slice.29), channel_id=1, replica_groups=mesh['blk'=4,'group'=8] {'blk'}, use_global_device_ids=true, to_apply=%add.3 | all-reduce | flops 32 | bytes 256
  70.6 5.2 %all_gather.35 = s32[32,16]{1,0:T(8,128)S(1)} all-gather(s32[8,16]{1,0:T(8,128)S(1)} %bitcast.189), channel_id=1, replica_groups=mesh['blk'=4,'group'=8] {'blk'}, dimensions={0}, use_global_device_ids=true | all-gather | bytes 2560 | tf_op jit(solution)/shard_map/all_gather | solution.py:128
  76.0 0.8 fusion.54
  77.1 0.8 dynamic-update-slice.30
  77.9 38.3 %all-reduce.5 = (f32[1024]{0:T(1024)S(1)}, f32[1024]{0:T(1024)S(1)}, f32[32]{0:T(128)S(1)}) all-reduce(f32[1024]{0:T(1024)S(1)} %dynamic-update-slice.26, f32[1024]{0:T(1024)S(1)} %dynamic-update-slice.27, f32[32]{0:T(128)S(1)} %dynamic-update-slice.30), channel_id=2, replica_groups=mesh['blk'=4,'group'=8] {'blk','group'}, use_global_device_ids=true, to_apply=%add | all-reduce | flops 2080 | bytes 16640
  116.4 40.0 %while.48 = (s32[]{:T(128)}, f32[32]{0:T(128)S(1)}, f32[32]{0:T(128)S(1)}, f32[]{:T(128)}, f32[32,32]{1,0:T(8,128)S(1)}, /*index=5*/f32[32,32]{1,0:T(8,128)S(1)}, f32[32]{0:T(128)S(1)}, s32[]{:T(128)}, s32[]{:T(128)}, s32[]{:T(128)}) while((s32[]{:T(128)}, f32[32]{0:T(128)S(1)}, f32[32]{0:T(128)S(1)}, f32[]{:T(128)}, ...), condition=%wide.region_10.11_spmd, body=%wide.region_9.10_spmd.sunk | while | flops 198 | bytes 939 | solution.py:39
  116.4 0.6 dynamic_slice.91
  117.7 0.6 dynamic_slice.91
  119.0 0.6 dynamic_slice.91
  120.3 0.6 dynamic_slice.91
  121.6 0.6 dynamic_slice.91
  122.9 0.6 dynamic_slice.91
  124.2 0.6 dynamic_slice.91
  125.5 0.6 dynamic_slice.91
  126.8 0.6 dynamic_slice.91
  128.1 0.6 dynamic_slice.91
  129.3 0.6 dynamic_slice.91
  130.6 0.6 dynamic_slice.91
  131.9 0.6 dynamic_slice.91
  133.2 0.6 dynamic_slice.91
  134.5 0.6 dynamic_slice.91
  135.8 0.6 dynamic_slice.91
  137.1 0.6 dynamic_slice.91
  138.4 0.6 dynamic_slice.91
  139.7 0.6 dynamic_slice.91
  141.0 0.6 dynamic_slice.91
  144.8 0.6 dynamic_slice.91
  156.4 0.6 fusion.56
  157.4 13.9 %while.49 = (s32[]{:T(128)}, bf16[8,16,128]{2,1,0:T(8,128)(2,1)S(1)}, f32[8,16,128]{2,1,0:T(8,128)S(1)}, f32[2,128,128]{2,1,0:T(8,128)S(1)}, s32[]{:T(128)}, /*i...) while((s32[]{:T(128)}, ...), condition=%wide.region_12.13_spmd, body=%wide.region_11.12_spmd.sunk | while | flops 25395472 | bytes 1589896 | solution.py:192
  158.3 2.4 collective-permute-start.1
  161.1 0.9 collective-permute-done.1
  163.0 2.4 collective-permute-start.1
  165.8 0.9 collective-permute-done.1
  167.6 2.4 collective-permute-start.1
  170.4 0.9 collective-permute-done.1
  172.9 2.8 %collective-permute-done.5 = f32[8,16,128]{2,1,0:T(8,128)S(1)} collective-permute-done((f32[8,16,128]{2,1,0:T(8,128)S(1)}, f32[8,16,128]{2,1,0:T(8,128)S(1)}, u32[]{:S(2)}, u32[]{:S(2)}) %collective-permute-start.5) | collective-permute-done | bytes 65568 | tf_op jit(solution)/shard_map/ppermute | solution.py:47
  175.7 0.6 copy-done.2
  176.5 63.4 %reduce-scatter.2.cloned.1.call-done = f32[1,16,128]{2,1,0:T(8,128)} async-done(((f32[8,16,128]{2,1,0:T(8,128)}), f32[1,16,128]{2,1,0:T(8,128)}) %reduce-scatter.2.cloned.1.call-update) | async-done | bytes 8208 | tf_op jit(solution)/shard_map/reduce_scatter | solution.py:197
  (161 shorter events, 14.4 us)
Async XLA Ops:
  7.2 0.7 copy-start.5
  7.2 232.7 %reduce-scatter.2.cloned.1.call-start = ((), (), s32[]{:S(2)}) async-start(), calls=%async_computation.1 | async-start | bytes 73728 | tf_op jit(solution)/shard_map/reduce_scatter | solution.py:197
  7.8 3.0 %copy-start.3 = (s32[2,128]{1,0:T(2,128)S(1)}, s32[2,128]{1,0:T(2,128)}, u32[]{:S(2)}) copy-start(s32[2,128]{1,0:T(2,128)} %param.21) | copy-start | bytes 3076
  7.8 44.4 %collective-permute-start.2 = (s32[1,1,16]{2,1,0:T(1,128)S(1)}, s32[1,1,16]{2,1,0:T(1,128)S(1)}, u32[]{:S(2)}, u32[]{:S(2)}) collective-permute-start(s32[1,1,16]{2,1,0:T(1,128)S(1)} %bitcast.196), channel_id=1, source_target_pairs={{0,1},{1,0},{2,3},{3,2},{4,5},{5,4},{6,7},{7,6},{8,9},{9,8},{10,11... | collective-permute-start | bytes 200 | tf_op jit(solution)/shard_map/ppermute | solution.py:22
  10.9 0.7 copy-start.4
  42.6 5.5 %copy-start.1 = (bf16[2,128,128]{2,1,0:T(8,128)(2,1)S(1)}, bf16[2,128,128]{2,1,0:T(8,128)(2,1)}, u32[]{:S(2)}) copy-start(bf16[2,128,128]{2,1,0:T(8,128)(2,1)} %param.20) | copy-start | bytes 196612
  48.9 0.7 copy-start.7
  50.2 0.7 copy-start.6
  52.3 10.6 %collective-permute-start.3 = (s32[2,1,16]{2,0,1:T(2,128)S(1)}, s32[2,1,16]{2,0,1:T(2,128)S(1)}, u32[]{:S(2)}, u32[]{:S(2)}) collective-permute-start(s32[2,1,16]{2,0,1:T(2,128)S(1)} %bitcast.192), channel_id=1, source_target_pairs={{0,2},{1,3},{2,0},{3,1},{4,6},{5,7},{6,4},{7,5},{8,10},{9,11},{10,... | collective-permute-start | bytes 392 | tf_op jit(solution)/shard_map/ppermute | solution.py:22
  62.9 7.7 %collective-permute-start.4 = (s32[4,1,16]{2,0,1:T(4,128)S(1)}, s32[4,1,16]{2,0,1:T(4,128)S(1)}, u32[]{:S(2)}, u32[]{:S(2)}) collective-permute-start(s32[4,1,16]{2,0,1:T(4,128)S(1)} %bitcast.190), channel_id=1, source_target_pairs={{0,4},{1,5},{2,6},{3,7},{4,0},{5,1},{6,2},{7,3},{8,12},{9,13},{10,... | collective-permute-start | bytes 776 | tf_op jit(solution)/shard_map/ppermute | solution.py:22
  157.4 3.7 %collective-permute-start = (bf16[8,16,128]{2,1,0:T(8,128)(2,1)S(1)}, bf16[8,16,128]{2,1,0:T(8,128)(2,1)S(1)}, u32[]{:S(2)}, u32[]{:S(2)}) collective-permute-start(bf16[8,16,128]{2,1,0:T(8,128)(2,1)S(1)} %copy.33), channel_id=1, source_target_pairs={{0,8},{8,16},{16,24},{24,0},{1,9},{9,17},{17,25},{25,1},{2,10},{10... | collective-permute-start | bytes 98312 | tf_op jit(solution)/shard_map/while/body/eval_jaxpr/ppermute | solution.py:47
  158.3 3.7 %collective-permute-start.1 = (f32[8,16,128]{2,1,0:T(8,128)S(1)}, f32[8,16,128]{2,1,0:T(8,128)S(1)}, u32[]{:S(2)}, u32[]{:S(2)}) collective-permute-start(f32[8,16,128]{2,1,0:T(8,128)S(1)} %add.311), channel_id=1, source_target_pairs={{0,8},{8,16},{16,24},{24,0},{1,9},{9,17},{17,25},{25,1},{2,10},{10... | collective-permute-start | bytes 196616 | tf_op jit(solution)/shard_map/while/body/eval_jaxpr/ppermute | solution.py:47
  162.1 3.7 %collective-permute-start = (bf16[8,16,128]{2,1,0:T(8,128)(2,1)S(1)}, bf16[8,16,128]{2,1,0:T(8,128)(2,1)S(1)}, u32[]{:S(2)}, u32[]{:S(2)}) collective-permute-start(bf16[8,16,128]{2,1,0:T(8,128)(2,1)S(1)} %copy.33), channel_id=1, source_target_pairs={{0,8},{8,16},{16,24},{24,0},{1,9},{9,17},{17,25},{25,1},{2,10},{10... | collective-permute-start | bytes 98312 | tf_op jit(solution)/shard_map/while/body/eval_jaxpr/ppermute | solution.py:47
  163.0 3.7 %collective-permute-start.1 = (f32[8,16,128]{2,1,0:T(8,128)S(1)}, f32[8,16,128]{2,1,0:T(8,128)S(1)}, u32[]{:S(2)}, u32[]{:S(2)}) collective-permute-start(f32[8,16,128]{2,1,0:T(8,128)S(1)} %add.311), channel_id=1, source_target_pairs={{0,8},{8,16},{16,24},{24,0},{1,9},{9,17},{17,25},{25,1},{2,10},{10... | collective-permute-start | bytes 196616 | tf_op jit(solution)/shard_map/while/body/eval_jaxpr/ppermute | solution.py:47
  166.7 3.6 %collective-permute-start = (bf16[8,16,128]{2,1,0:T(8,128)(2,1)S(1)}, bf16[8,16,128]{2,1,0:T(8,128)(2,1)S(1)}, u32[]{:S(2)}, u32[]{:S(2)}) collective-permute-start(bf16[8,16,128]{2,1,0:T(8,128)(2,1)S(1)} %copy.33), channel_id=1, source_target_pairs={{0,8},{8,16},{16,24},{24,0},{1,9},{9,17},{17,25},{25,1},{2,10},{10... | collective-permute-start | bytes 98312 | tf_op jit(solution)/shard_map/while/body/eval_jaxpr/ppermute | solution.py:47
  167.6 3.7 %collective-permute-start.1 = (f32[8,16,128]{2,1,0:T(8,128)S(1)}, f32[8,16,128]{2,1,0:T(8,128)S(1)}, u32[]{:S(2)}, u32[]{:S(2)}) collective-permute-start(f32[8,16,128]{2,1,0:T(8,128)S(1)} %add.311), channel_id=1, source_target_pairs={{0,8},{8,16},{16,24},{24,0},{1,9},{9,17},{17,25},{25,1},{2,10},{10... | collective-permute-start | bytes 196616 | tf_op jit(solution)/shard_map/while/body/eval_jaxpr/ppermute | solution.py:47
  171.9 3.7 %collective-permute-start.5 = (f32[8,16,128]{2,1,0:T(8,128)S(1)}, f32[8,16,128]{2,1,0:T(8,128)S(1)}, u32[]{:S(2)}, u32[]{:S(2)}) collective-permute-start(f32[8,16,128]{2,1,0:T(8,128)S(1)} %add.250), channel_id=1, source_target_pairs={{0,8},{8,16},{16,24},{24,0},{1,9},{9,17},{17,25},{25,1},{2,10},{10... | collective-permute-start | bytes 196616 | tf_op jit(solution)/shard_map/ppermute | solution.py:47
  175.7 0.6 copy-start.2
  176.5 63.4 %copy-start = (f32[2,128,128]{2,1,0:T(8,128)}, f32[2,128,128]{2,1,0:T(8,128)S(1)}, u32[]{:S(2)}) copy-start(f32[2,128,128]{2,1,0:T(8,128)S(1)} %fusion.38) | copy-start | bytes 393220
Sparse Core Ops, SparseCore 0:
  176.5 63.3 reduce-scatter.1
